TPU v7x, 512 devices: a whole 4x8x8 slice. The times are simulated.
512 devices in a mesh: frames: 32 (over x, y_lo, core), book: 16 (over z, y_hi).
Axes of the slice: x: 4, y: 8 (y_hi: 2, y_lo: 4; y = y_hi * 4 + y_lo), z: 8, core: 2. Of those that a mesh axis runs over, the one named last changes fastest.
Arguments:
- gate_pre: bfloat16 [8192, 6144], P('frames', 'book'), may hold values from -6 to 6
- up_pre: bfloat16 [8192, 6144], P('frames', 'book'), may hold values from -6 to 6
- down_weight: bfloat16 [6144, 4096], P('book'), may hold values from -0.109375 to 0.109375
- residual: bfloat16 [8192, 4096], P('frames', 'book'), may hold values from -6 to 6
- out_gain: bfloat16 [4096], replicated, may hold values from 0.25 to 1.75
- in_proj: bfloat16 [16, 4096, 1024], P('book', 'frames'), may hold values from -0.09375 to 0.09375
- embedding: bfloat16 [16, 1024, 1024], P('book', 'frames'), may hold values from -6 to 6
- token_ids: int32 [8192, 16], P('frames', 'book'), may hold values from 0 to 1023
- depth_gain: bfloat16 [16, 1024], P('book'), may hold values from 0.25 to 1.75
- qkv_weight: bfloat16 [16, 1024, 1536], P('book', 'frames'), may hold values from -2 to 2
Outputs:
- context: bfloat16 [8192, 16, 512], P(('frames', 'book'))
All inputs are finite; a program needn't handle non-finite values.
Results may differ from a plain program's by a relative error of at most 0.019.
Values may be sent and summed in bfloat16 or wider, within the bound.
A program may use at most 64 MiB of HBM per device.

v0:
```python
import jax
import jax.numpy as jnp
from jax import lax
from jax.sharding import Mesh
from jax.sharding import PartitionSpec as P

H = 8
HD = 64
BOOK = ("book_0", "book_1")
FRAMES_BOOK = ("frames", "book_0", "book_1")


def sum_by_axis(shard, axes, dim):
    if not axes:
        return shard
    nearer = lax.psum_scatter(shard, axes[0], scatter_dimension=dim, tiled=True)
    return sum_by_axis(nearer, axes[1:], dim)


def rms_scale(values, gain):
    moment = jnp.mean(values * values, axis=-1, keepdims=True)
    return values * lax.rsqrt(moment + 1e-05) * gain


def attend_block(grouped):
    inner = grouped[0]
    frames_here = inner.shape[0]
    books = inner.shape[1]
    width = H * HD
    queries = inner[:, :, :width].reshape(frames_here, books, H, HD)
    keys_all = inner[:, :, width : 2 * width].reshape(frames_here, books, H, HD)
    values_all = inner[:, :, 2 * width :].reshape(frames_here, books, H, HD)
    scores = jnp.einsum(
        "nkhd,njhd->nhkj", queries, keys_all, preferred_element_type=jnp.float32
    ) * HD ** (-0.5)
    causal = lax.broadcasted_iota(jnp.int32, (books, books), 0) >= lax.broadcasted_iota(
        jnp.int32, (books, books), 1
    )
    scores = jnp.where(causal, scores, -1e30)
    peak = jnp.max(scores, axis=-1, keepdims=True)
    expo = jnp.exp(scores - peak)
    probability = (expo / jnp.sum(expo, axis=-1, keepdims=True)).astype(jnp.bfloat16)
    context = jnp.einsum(
        "nhkj,njhd->nkhd", probability, values_all, preferred_element_type=jnp.float32
    )
    return context.reshape(1, frames_here, books, width).astype(jnp.bfloat16)


def gather_embedding(embedding, token_column):
    table_piece = lax.all_gather(embedding, "frames", axis=1, tiled=True)
    columns = lax.broadcasted_iota(jnp.int32, (1, table_piece.shape[1]), 1)
    matches = (token_column[:, None] == columns).astype(jnp.bfloat16)
    return jnp.dot(matches, table_piece[0], preferred_element_type=jnp.float32)


def per_device(
    gate_pre,
    up_pre,
    down_weight,
    residual,
    out_gain,
    in_proj,
    embedding,
    token_ids,
    depth_gain,
    qkv_weight,
):
    tokens_here = gate_pre.shape[0]
    book_count = lax.axis_size(BOOK)
    token_column = token_ids[:, 0]
    hidden = (jax.nn.silu(gate_pre.astype(jnp.float32)) * up_pre.astype(jnp.float32)).astype(
        jnp.bfloat16
    )
    partial_value = jnp.dot(hidden, down_weight, preferred_element_type=jnp.float32)
    share = sum_by_axis(partial_value, BOOK, 1)
    temporal = (share + residual.astype(jnp.float32)).astype(jnp.bfloat16)
    whole = lax.all_gather(temporal, BOOK, axis=1, tiled=True)
    normed = rms_scale(whole.astype(jnp.float32), out_gain.astype(jnp.float32)).astype(jnp.bfloat16)
    looked = gather_embedding(embedding, token_column)
    columns = normed
    projected = jnp.dot(
        columns,
        lax.all_gather(in_proj, "frames", axis=1, tiled=True)[0],
        preferred_element_type=jnp.float32,
    )
    depth_in = (projected + looked).astype(jnp.bfloat16)
    depth_normed = rms_scale(
        depth_in.astype(jnp.float32), depth_gain[0].astype(jnp.float32)
    ).astype(jnp.bfloat16)
    columns = depth_normed
    packed = jnp.dot(
        columns,
        lax.all_gather(qkv_weight, "frames", axis=1, tiled=True)[0],
        preferred_element_type=jnp.float32,
    ).astype(jnp.bfloat16)
    grouped = packed.reshape(book_count, tokens_here // book_count, 1, packed.shape[1])
    context = attend_block(lax.all_to_all(grouped, BOOK, split_axis=0, concat_axis=2, tiled=True))
    return context.reshape(context.shape[1], context.shape[2], context.shape[3])


def solution(mesh):
    split = Mesh(mesh.devices.reshape(mesh.shape["frames"], 8, 2), ("frames", "book_0", "book_1"))
    placed = (
        P("frames", BOOK),
        P("frames", BOOK),
        P(BOOK, None),
        P("frames", BOOK),
        P(),
        P(BOOK, "frames", None),
        P(BOOK, "frames", None),
        P("frames", BOOK),
        P(BOOK, None),
        P(BOOK, "frames", None),
    )
    return jax.shard_map(
        per_device,
        mesh=split,
        in_specs=placed,
        out_specs=P(FRAMES_BOOK, None, None),
        check_vma=False,
    )
```

profile of v0, /device:TPU:40, one launch (start us, length us, event | category | flops | bytes accessed | tf_op | source)
XLA Modules:
  0.0 474.8 jit_solution(13796978290205377564)
XLA Ops:
  6.5 1.9 copy-done
  8.4 4.3 fusion.42
  12.8 63.1 %reduce-scatter.3.cloned.1.call-done = f32[256,512]{1,0:T(8,128)} async-done(((f32[256,4096]{1,0:T(8,128)}), f32[256,512]{1,0:T(8,128)}) %reduce-scatter.3.cloned.1.call-update) | async-done | bytes 524304 | tf_op jit(solution)/shard_map/reduce_scatter | solution.py:16
  75.9 28.9 %reduce-scatter.5.cloned.1.call-done = f32[256,256]{1,0:T(8,128)} async-done(((f32[256,512]{1,0:T(8,128)}), f32[256,256]{1,0:T(8,128)}) %reduce-scatter.5.cloned.1.call-update) | async-done | bytes 262160 | tf_op jit(solution)/shard_map/reduce_scatter | solution.py:16
  104.8 1.6 add_convert_fusion
  107.0 0.5 all-gather.9.cloned.1.call-update
  108.2 101.6 %all-gather.5.cloned.1.call-done = bf16[256,4096]{1,0:T(8,128)(2,1)} async-done(((bf16[256,256]{1,0:T(8,128)(2,1)}), bf16[256,4096]{1,0:T(8,128)(2,1)}) %all-gather.5.cloned.1.call-update) | async-done | bytes 2097168 | tf_op jit(solution)/shard_map/all_gather | solution.py:77
  209.8 2.1 fusion.3
  211.9 68.1 %all-gather.7.cloned.1.call-done = bf16[1,4096,1024]{2,1,0:T(8,128)(2,1)} async-done(((bf16[1,128,1024]{2,1,0:T(8,128)(2,1)}), bf16[1,4096,1024]{2,1,0:T(8,128)(2,1)}) %all-gather.7.cloned.1.call-update) | async-done | bytes 8388624 | tf_op jit(solution)/shard_map/all_gather | solution.py:83
  280.0 7.4 %fusion.1 = f32[256,1024]{1,0:T(8,128)} fusion(bf16[1,4096,1024]{2,1,0:T(8,128)(2,1)} %all-gather.7.cloned.1.call-done, bf16[256,4096]{1,0:T(8,128)(2,1)} %all-gather.5.cloned.1.call-done, f32[4096]{0:T(1024)S(1)} %convert_element_type.60, f32[256]{0:T(256)S(1)} %add_rsqrt_fusion.1), kind=kOutput, calls=%fused_computation.1 | convolution fusion | flops 2151677952 | bytes 11551744 | tf_op jit(solution)/shard_map/dot_general | solution.py:81
  287.4 55.8 %all-gather.9.cloned.1.call-done = bf16[1,1024,1024]{2,1,0:T(8,128)(2,1)} async-done(((bf16[1,32,1024]{2,1,0:T(8,128)(2,1)}), bf16[1,1024,1024]{2,1,0:T(8,128)(2,1)}) %all-gather.9.cloned.1.call-update) | async-done | bytes 2097168 | tf_op jit(solution)/shard_map/all_gather | solution.py:50
  343.2 3.4 fusion.26
  346.6 61.3 %all-gather.11.cloned.1.call-done = bf16[1,1024,1536]{2,1,0:T(8,128)(2,1)} async-done(((bf16[1,32,1536]{2,1,0:T(8,128)(2,1)}), bf16[1,1024,1536]{2,1,0:T(8,128)(2,1)}) %all-gather.11.cloned.1.call-update) | async-done | bytes 3145744 | tf_op jit(solution)/shard_map/all_gather | solution.py:93
  407.9 4.0 fusion.8
  411.9 12.8 %all-to-all-start = ((bf16[16,16,1,1536]{3,1,2,0:T(8,128)(2,1)}), bf16[16,16,1,1536]{3,1,2,0:T(8,128)(2,1)}, u32[]{:S(2)}, u32[]{:S(2)}) async-start(bf16[16,16,1,1536]{3,1,2,0:T(8,128)(2,1)} %bitcast.38), calls=%async_computation.2 | async-start | bytes 1572864 | tf_op jit(solution)/shard_map/all_to_all | solution.py:97
  424.7 28.0 %all-to-all-done = bf16[16,16,1,1536]{3,1,2,0:T(8,128)(2,1)} async-done(((bf16[16,16,1,1536]{3,1,2,0:T(8,128)(2,1)}), bf16[16,16,1,1536]{3,1,2,0:T(8,128)(2,1)}, u32[]{:S(2)}, u32[]{:S(2)}) %all-to-all-start) | async-done | bytes 786464 | tf_op jit(solution)/shard_map/all_to_all | solution.py:97
  452.6 2.0 fusion.46
  454.6 2.1 reshape.45
  456.7 2.1 reshape.46
  458.8 1.1 reshape.44
  459.9 3.2 fusion.47
  463.0 1.9 fusion.25
  464.9 0.9 copy.26
  465.9 2.1 convert_element_type.69
  (25 shorter events, 1.3 us)
Async XLA Ops:
  6.5 1.9 copy-start
  6.5 69.3 %reduce-scatter.3.cloned.1.call-start = ((), (), s32[]{:S(2)}) async-start(), calls=%async_computation.3 | async-start | bytes 4718592 | tf_op jit(solution)/shard_map/reduce_scatter | solution.py:16
  12.7 92.1 %copy-start.1 = (bf16[256,256]{1,0:T(8,128)(2,1)S(1)}, bf16[256,256]{1,0:T(8,128)(2,1)}, u32[]{:S(2)}) copy-start(bf16[256,256]{1,0:T(8,128)(2,1)} %param.13) | copy-start | bytes 393220
  12.7 95.5 %copy-start.2 = (bf16[4096]{0:T(1024)(128)(2,1)S(1)}, bf16[4096]{0:T(1024)(128)(2,1)}, u32[]{:S(2)}) copy-start(bf16[4096]{0:T(1024)(128)(2,1)} %param.14) | copy-start | bytes 24580
  12.7 95.5 %copy-start.3 = (bf16[1,1024]{1,0:T(2,128)(2,1)S(1)}, bf16[1,1024]{1,0:T(2,128)(2,1)}, u32[]{:S(2)}) copy-start(bf16[1,1024]{1,0:T(2,128)(2,1)} %param.18) | copy-start | bytes 6148
  12.7 92.1 %reduce-scatter.5.cloned.1.call-start = ((), (), s32[]{:S(2)}) async-start(), calls=%async_computation.4 | async-start | bytes 786432 | tf_op jit(solution)/shard_map/reduce_scatter | solution.py:16
  75.8 133.9 %all-gather.5.cloned.1.call-start = ((), (), s32[]{:S(2)}) async-start(), calls=%async_computation.5 | async-start | bytes 2228224 | tf_op jit(solution)/shard_map/all_gather | solution.py:77
  106.4 173.6 %all-gather.7.cloned.1.call-start = ((), (), s32[]{:S(2)}) async-start(), calls=%async_computation.6 | async-start | bytes 8650752 | tf_op jit(solution)/shard_map/all_gather | solution.py:83
  107.0 236.2 %all-gather.9.cloned.1.call-start = ((), (), s32[]{:S(2)}) async-start(), calls=%async_computation.7 | async-start | bytes 2162688 | tf_op jit(solution)/shard_map/all_gather | solution.py:50
  107.6 300.3 %all-gather.11.cloned.1.call-start = ((), (), s32[]{:S(2)}) async-start(), calls=%async_computation.8 | async-start | bytes 3244032 | tf_op jit(solution)/shard_map/all_gather | solution.py:93
  211.9 131.3 %copy-start.4 = (s32[256,1]{0,1:T(1,128)S(1)}, s32[256,1]{0,1:T(1,128)}, u32[]{:S(2)}) copy-start(s32[256,1]{0,1:T(1,128)} %param.17) | copy-start | bytes 3076
  411.9 40.7 %all-to-all-start = ((bf16[16,16,1,1536]{3,1,2,0:T(8,128)(2,1)}), bf16[16,16,1,1536]{3,1,2,0:T(8,128)(2,1)}, u32[]{:S(2)}, u32[]{:S(2)}) async-start(bf16[16,16,1,1536]{3,1,2,0:T(8,128)(2,1)} %bitcast.38), calls=%async_computation.2 | async-start | bytes 1572864 | tf_op jit(solution)/shard_map/all_to_all | solution.py:97
Sparse Core Ops, SparseCore 0:
  12.8 62.9 reduce-scatter.2
  78.6 26.1 reduce-scatter.4
  107.8 101.8 all-gather.4
  211.8 68.1 all-gather.6
  282.0 61.1 all-gather.8
  345.2 62.6 all-gather.10
where the time goes:
time: 475 us
  waiting for transfers between devices  408 us (86%)
  matrix products  24.1 us (5%)
  between operations  13.5 us (3%)
  starting transfers between devices  13 us (3%)
  local copies, waits for them, and re-layouts  12.1 us (3%)
    all_gather x1, waiting for transfers between devices, per_device(): whole = lax.all_gather(temporal, BOOK, axis=1, tiled=True)  102 us
    reduce_scatter x2, waiting for transfers between devices, sum_by_axis(): nearer = lax.psum_scatter(shard, axes[0], scatter_dimension=dim, tiled=True)  91.9 us
    all_gather x1, waiting for transfers between devices, per_device(): lax.all_gather(in_proj, 'frames', axis=1, tiled=True)[0]  68.1 us
    all_gather x1, waiting for transfers between devices, per_device(): lax.all_gather(qkv_weight, 'frames', axis=1, tiled=True)[0]  61.3 us
    all_gather x1, waiting for transfers between devices, gather_embedding(): table_piece = lax.all_gather(embedding, 'frames', axis=1, tiled=True)  55.8 us
    all_to_all x1, waiting for transfers between devices, per_device(): lax.all_to_all(grouped, BOOK, split_axis=0, concat_axis=2, tiled=True)  28 us
    all_to_all x1, starting transfers between devices, per_device(): lax.all_to_all(grouped, BOOK, split_axis=0, concat_axis=2, tiled=True)  12.8 us
  transfers between devices with their start and end apart: 7, of which 7 were waited for; matrix products, arithmetic and copies ran while one was open for 3% of the time, Pallas kernels for 0%

commit v1 on v0

--- a/solution.py
+++ b/solution.py
@@ -74,7 +74,9 @@
     partial_value = jnp.dot(hidden, down_weight, preferred_element_type=jnp.float32)
     share = sum_by_axis(partial_value, BOOK, 1)
     temporal = (share + residual.astype(jnp.float32)).astype(jnp.bfloat16)
-    whole = lax.all_gather(temporal, BOOK, axis=1, tiled=True)
+    whole = jnp.concatenate(
+        lax.all_to_all(jnp.stack([temporal] * lax.axis_size(BOOK)), BOOK, 0, 0), axis=1
+    )
     normed = rms_scale(whole.astype(jnp.float32), out_gain.astype(jnp.float32)).astype(jnp.bfloat16)
     looked = gather_embedding(embedding, token_column)
     columns = normed

time: 475 us -> 409 us (0.86)
  waiting for transfers between devices: 408 us -> 324 us
  starting transfers between devices: 13 us -> 25.7 us
    all_gather x1 -> x0, waiting for transfers between devices: 102 us -> none  [per_device(): whole = lax.all_gather(temporal, BOOK, axis=1, tiled=True)]
    all_to_all x0 -> x1, waiting for transfers between devices: none -> 68.8 us  [per_device(): lax.all_to_all(jnp.stack([temporal] * lax.axis_size(BOOK)), BOOK, 0, 0)]
    all_gather x1, waiting for transfers between devices: 68.1 us -> 4.79 us  [per_device(): lax.all_gather(in_proj, 'frames', axis=1, tiled=True)[0]]
    all_gather x1, waiting for transfers between devices: 55.8 us -> 69 us  [gather_embedding(): table_piece = lax.all_gather(embedding, 'frames', axis=1, tiled=True)]
    all_to_all x0 -> x1, starting transfers between devices: none -> 12.7 us  [per_device(): lax.all_to_all(jnp.stack([temporal] * lax.axis_size(BOOK)), BOOK, 0, 0)]
  transfers between devices with their start and end apart: 7 -> 7, of which waited for: 7 -> 7; matrix products, arithmetic and copies ran while one was open for 3% -> 5% of each run, Pallas kernels for 0% -> 0%
where the time goes in v1:
time: 409 us
  waiting for transfers between devices  324 us (79%)
  starting transfers between devices  25.7 us (6%)
  matrix products  24.1 us (6%)
  between operations  15.1 us (4%)
  local copies, waits for them, and re-layouts  13.7 us (3%)
  other arithmetic  6.13 us (1%)
    reduce_scatter x2, waiting for transfers between devices, sum_by_axis(): nearer = lax.psum_scatter(shard, axes[0], scatter_dimension=dim, tiled=True)  90.5 us
    all_gather x1, waiting for transfers between devices, gather_embedding(): table_piece = lax.all_gather(embedding, 'frames', axis=1, tiled=True)  69 us
    all_to_all x1, waiting for transfers between devices, per_device(): lax.all_to_all(jnp.stack([temporal] * lax.axis_size(BOOK)), BOOK, 0, 0)  68.8 us
    all_gather x1, waiting for transfers between devices, per_device(): lax.all_gather(qkv_weight, 'frames', axis=1, tiled=True)[0]  61.4 us
    all_to_all x1, waiting for transfers between devices, per_device(): lax.all_to_all(grouped, BOOK, split_axis=0, concat_axis=2, tiled=True)  27.8 us
    all_to_all x1, starting transfers between devices, per_device(): lax.all_to_all(grouped, BOOK, split_axis=0, concat_axis=2, tiled=True)  12.8 us
    all_to_all x1, starting transfers between devices, per_device(): lax.all_to_all(jnp.stack([temporal] * lax.axis_size(BOOK)), BOOK, 0, 0)  12.7 us
  transfers between devices with their start and end apart: 7, of which 7 were waited for; matrix products, arithmetic and copies ran while one was open for 5% of the time, Pallas kernels for 0%

profile of v1, /device:TPU:40, one launch (start us, length us, event | category | flops | bytes accessed | tf_op | source)
XLA Modules:
  0.0 408.6 jit_solution(712892694039130844)
XLA Ops:
  7.4 1.9 copy-done
  9.3 4.3 %fusion.39 = f32[256,4096]{1,0:T(8,128)} fusion(bf16[384,4096]{1,0:T(8,128)(2,1)S(1)} %copy-done, bf16[256,384]{1,0:T(8,128)(2,1)} %param.11, bf16[256,384]{1,0:T(8,128)(2,1)} %param.10), kind=kOutput, calls=%fused_computation.43 | convolution fusion | flops 806092800 | bytes 7733248 | tf_op jit(solution)/shard_map/dot_general | solution.py:74
  13.6 63.1 %reduce-scatter.3.cloned.1.call-done = f32[256,512]{1,0:T(8,128)} async-done(((f32[256,4096]{1,0:T(8,128)}), f32[256,512]{1,0:T(8,128)}) %reduce-scatter.3.cloned.1.call-update) | async-done | bytes 524304 | tf_op jit(solution)/shard_map/reduce_scatter | solution.py:16
  78.4 27.5 %reduce-scatter.5.cloned.1.call-done = f32[256,256]{1,0:T(8,128)} async-done(((f32[256,512]{1,0:T(8,128)}), f32[256,256]{1,0:T(8,128)}) %reduce-scatter.5.cloned.1.call-update) | async-done | bytes 262160 | tf_op jit(solution)/shard_map/reduce_scatter | solution.py:16
  107.0 1.5 stack.2
  108.5 12.7 %all-to-all-start = ((bf16[16,256,256]{1,2,0:T(8,128)(2,1)}), bf16[16,256,256]{1,2,0:T(8,128)(2,1)}, u32[]{:S(2)}, u32[]{:S(2)}) async-start(bf16[16,256,256]{1,2,0:T(8,128)(2,1)} %stack.2), calls=%async_computation.2 | async-start | bytes 4194304 | tf_op jit(solution)/shard_map/all_to_all | solution.py:78
  121.3 68.8 %all-to-all-done = bf16[16,256,256]{1,2,0:T(8,128)(2,1)} async-done(((bf16[16,256,256]{1,2,0:T(8,128)(2,1)}), bf16[16,256,256]{1,2,0:T(8,128)(2,1)}, u32[]{:S(2)}, u32[]{:S(2)}) %all-to-all-start) | async-done | bytes 2097184 | tf_op jit(solution)/shard_map/all_to_all | solution.py:78
  190.1 2.2 fusion.3
  192.3 2.9 fusion.5
  195.2 4.8 %all-gather.4.cloned.1.call-done = bf16[1,4096,1024]{2,1,0:T(8,128)(2,1)} async-done(((bf16[1,128,1024]{2,1,0:T(8,128)(2,1)}), bf16[1,4096,1024]{2,1,0:T(8,128)(2,1)}) %all-gather.4.cloned.1.call-update) | async-done | bytes 8388624 | tf_op jit(solution)/shard_map/all_gather | solution.py:85
  200.0 7.4 %fusion.1 = f32[256,1024]{1,0:T(8,128)} fusion(bf16[256,4096]{0,1:T(8,128)(2,1)} %bitcast.42, bf16[1,4096,1024]{2,1,0:T(8,128)(2,1)} %all-gather.4.cloned.1.call-done), kind=kOutput, calls=%fused_computation.1 | convolution fusion | flops 2147483648 | bytes 11534336 | tf_op jit(solution)/shard_map/dot_general | solution.py:83
  207.4 69.0 %all-gather.6.cloned.1.call-done = bf16[1,1024,1024]{2,1,0:T(8,128)(2,1)} async-done(((bf16[1,32,1024]{2,1,0:T(8,128)(2,1)}), bf16[1,1024,1024]{2,1,0:T(8,128)(2,1)}) %all-gather.6.cloned.1.call-update) | async-done | bytes 2097168 | tf_op jit(solution)/shard_map/all_gather | solution.py:50
  276.4 3.4 fusion.23
  279.9 61.4 %all-gather.8.cloned.1.call-done = bf16[1,1024,1536]{2,1,0:T(8,128)(2,1)} async-done(((bf16[1,32,1536]{2,1,0:T(8,128)(2,1)}), bf16[1,1024,1536]{2,1,0:T(8,128)(2,1)}) %all-gather.8.cloned.1.call-update) | async-done | bytes 3145744 | tf_op jit(solution)/shard_map/all_gather | solution.py:95
  341.2 4.0 fusion.8
  345.2 12.8 %all-to-all-start.1 = ((bf16[16,16,1,1536]{3,1,2,0:T(8,128)(2,1)}), bf16[16,16,1,1536]{3,1,2,0:T(8,128)(2,1)}, u32[]{:S(2)}, u32[]{:S(2)}) async-start(bf16[16,16,1,1536]{3,1,2,0:T(8,128)(2,1)} %bitcast.43), calls=%async_computation.3 | async-start | bytes 1572864 | tf_op jit(solution)/shard_map/all_to_all | solution.py:99
  358.0 27.8 %all-to-all-done.1 = bf16[16,16,1,1536]{3,1,2,0:T(8,128)(2,1)} async-done(((bf16[16,16,1,1536]{3,1,2,0:T(8,128)(2,1)}), bf16[16,16,1,1536]{3,1,2,0:T(8,128)(2,1)}, u32[]{:S(2)}, u32[]{:S(2)}) %all-to-all-start.1) | async-done | bytes 786464 | tf_op jit(solution)/shard_map/all_to_all | solution.py:99
  385.7 1.9 fusion.43
  387.7 2.1 reshape.62
  389.8 2.1 reshape.63
  391.8 1.1 reshape.61
  392.9 3.2 fusion.44
  396.1 1.9 fusion.22
  398.9 2.1 convert_element_type.77
  (27 shorter events, 3.9 us)
Async XLA Ops:
  7.4 1.9 copy-start
  7.4 69.3 %reduce-scatter.3.cloned.1.call-start = ((), (), s32[]{:S(2)}) async-start(), calls=%async_computation.4 | async-start | bytes 4718592 | tf_op jit(solution)/shard_map/reduce_scatter | solution.py:16
  13.5 92.4 %copy-start.1 = (bf16[256,256]{1,0:T(8,128)(2,1)S(1)}, bf16[256,256]{1,0:T(8,128)(2,1)}, u32[]{:S(2)}) copy-start(bf16[256,256]{1,0:T(8,128)(2,1)} %param.13) | copy-start | bytes 393220
  13.5 92.3 %reduce-scatter.5.cloned.1.call-start = ((), (), s32[]{:S(2)}) async-start(), calls=%async_computation.5 | async-start | bytes 786432 | tf_op jit(solution)/shard_map/reduce_scatter | solution.py:16
  76.7 123.4 %all-gather.4.cloned.1.call-start = ((), (), s32[]{:S(2)}) async-start(), calls=%async_computation.6 | async-start | bytes 8650752 | tf_op jit(solution)/shard_map/all_gather | solution.py:85
  77.3 199.2 %all-gather.6.cloned.1.call-start = ((), (), s32[]{:S(2)}) async-start(), calls=%async_computation.7 | async-start | bytes 2162688 | tf_op jit(solution)/shard_map/all_gather | solution.py:50
  77.8 263.4 %all-gather.8.cloned.1.call-start = ((), (), s32[]{:S(2)}) async-start(), calls=%async_computation.8 | async-start | bytes 3244032 | tf_op jit(solution)/shard_map/all_gather | solution.py:95
  107.0 14.3 %copy-start.2 = (bf16[4096]{0:T(1024)(128)(2,1)S(1)}, bf16[4096]{0:T(1024)(128)(2,1)}, u32[]{:S(2)}) copy-start(bf16[4096]{0:T(1024)(128)(2,1)} %param.14) | copy-start | bytes 24580
  107.0 14.3 %copy-start.3 = (bf16[1,1024]{1,0:T(2,128)(2,1)S(1)}, bf16[1,1024]{1,0:T(2,128)(2,1)}, u32[]{:S(2)}) copy-start(bf16[1,1024]{1,0:T(2,128)(2,1)} %param.18) | copy-start | bytes 6148
  108.5 81.6 %all-to-all-start = ((bf16[16,256,256]{1,2,0:T(8,128)(2,1)}), bf16[16,256,256]{1,2,0:T(8,128)(2,1)}, u32[]{:S(2)}, u32[]{:S(2)}) async-start(bf16[16,256,256]{1,2,0:T(8,128)(2,1)} %stack.2), calls=%async_computation.2 | async-start | bytes 4194304 | tf_op jit(solution)/shard_map/all_to_all | solution.py:78
  200.0 76.4 %copy-start.4 = (s32[256,1]{0,1:T(1,128)S(1)}, s32[256,1]{0,1:T(1,128)}, u32[]{:S(2)}) copy-start(s32[256,1]{0,1:T(1,128)} %param.17) | copy-start | bytes 3076
  345.2 40.5 %all-to-all-start.1 = ((bf16[16,16,1,1536]{3,1,2,0:T(8,128)(2,1)}), bf16[16,16,1,1536]{3,1,2,0:T(8,128)(2,1)}, u32[]{:S(2)}, u32[]{:S(2)}) async-start(bf16[16,16,1,1536]{3,1,2,0:T(8,128)(2,1)} %bitcast.43), calls=%async_computation.3 | async-start | bytes 1572864 | tf_op jit(solution)/shard_map/all_to_all | solution.py:99
Sparse Core Ops, SparseCore 0:
  13.7 62.9 reduce-scatter.2
  79.4 26.3 reduce-scatter.4
Sparse Core Ops, SparseCore 1:
  79.3 120.7 all-gather.3
  202.0 74.3 all-gather.5
  278.4 62.7 all-gather.7
